TPU v7x, 128 devices: a whole 4x4x4 slice. The times are simulated.
128 devices in a mesh: row: 16 (over z, x_lo, core), col: 8 (over y, x_hi).
Axes of the slice: x: 4 (x_hi: 2, x_lo: 2; x = x_hi * 2 + x_lo), y: 4, z: 4, core: 2. Of those that a mesh axis runs over, the one named last changes fastest.
Arguments:
- genotypes: bfloat16 [5120, 16384], P(None, ('row', 'col')), may hold values from -5 to 5
- running: float32 [16384, 16, 8, 128], P('row', None, 'col'), as said below
- grid_map: int32 [16], replicated, may hold values from 0 to 15, each once
Outputs:
- factored: float32 [16, 16, 64, 16, 8, 128], P(None, 'row', None, None, 'col')
Inputs may be any that keep to these rules, and one draw needn't show every extreme that they name: running is symmetric, and in its first 128 rows each diagonal entry exceeds the sum of the magnitudes of the row's other entries among the first 128 columns. grid_map holds each of its values once.
All inputs are finite; a program needn't handle non-finite values.
Results may differ from a plain program's by a relative error of at most 0.0003.
Values may be sent and summed in bfloat16 or wider, within the bound.
No kernel may reach another device: no remote copies, remote signals or barrier semaphores. Data moves between devices by JAX's collectives and lax.ppermute only.
A program may use at most 128 MiB of HBM per device.

v0:
```python
import jax
import jax.numpy as jnp
from jax import lax
from jax.sharding import PartitionSpec as P

NB = 128


def broadcast(array, axis, root):
    mine = lax.axis_index(axis) == root
    return lax.psum(jnp.where(mine, array, jnp.zeros_like(array)), axis)


def assemble(trail, row_factor, global_rows, col_index, col_width):
    col_pos = jnp.arange(col_width, dtype=jnp.int32)
    in_panel = jnp.logical_and(col_index == 0, col_pos < NB)
    padded = jnp.pad(row_factor, ((0, 0), (0, col_width - NB)))
    left_part = jnp.where(global_rows[:, None] >= col_pos[None, :], padded, jnp.zeros_like(padded))
    right_part = jnp.where(global_rows[:, None] < NB, jnp.zeros_like(trail), trail)
    return jnp.where(in_panel[None, :], left_part, right_part)


def on_device(genotypes, running, grid_map):
    rows_count = lax.axis_size("row")
    row_index = lax.axis_index("row")
    col_index = lax.axis_index("col")
    snp_count = genotypes.shape[0]
    shard_cols = running.shape[3]
    block_rows = running.shape[0]
    sub_rows = block_rows // rows_count
    col_width = running.shape[1] * shard_cols
    mine_rows = lax.all_gather(genotypes, "col", axis=1, tiled=True)
    product = lax.dot_general(
        mine_rows,
        lax.all_gather(genotypes, "row", axis=1, tiled=True),
        (((0,), (0,)), ((), ())),
        preferred_element_type=jnp.float32,
    )
    updated = running.reshape(block_rows, col_width) + product * (1.0 / snp_count)
    inverse_map = jnp.argsort(grid_map)
    leading = broadcast(updated[:NB, :NB], "row", 0)
    lower_factor = jnp.linalg.cholesky(leading)
    own_factor = lax.linalg.triangular_solve(
        lower_factor, updated[:, :NB], left_side=False, lower=True, transpose_a=True
    )
    factor_block = broadcast(own_factor, "col", 0)
    col_slice = lax.dynamic_slice_in_dim(factor_block, col_index * shard_cols, shard_cols, 0)
    col_factor = lax.all_gather(col_slice, "row", axis=0, tiled=True)
    trail = updated - jnp.dot(factor_block, col_factor.T, precision=lax.Precision.HIGHEST)
    global_rows = row_index * block_rows + jnp.arange(block_rows, dtype=jnp.int32)
    finished = assemble(trail, factor_block, global_rows, col_index, col_width)
    send_tiles = jnp.take(finished.reshape(rows_count, sub_rows, col_width), inverse_map, axis=0)
    result = lax.all_to_all(send_tiles, "row", split_axis=0, concat_axis=0, tiled=True)
    return result.reshape(rows_count, 1, sub_rows, rows_count, 1, shard_cols)


def solution(mesh):
    in_specs = (P(None, ("row", "col")), P("row", None, "col", None), P())
    out_specs = P(None, "row", None, None, "col", None)
    return jax.shard_map(
        on_device, mesh=mesh, in_specs=in_specs, out_specs=out_specs, check_vma=False
    )
```

profile of v0, /device:TPU:1, one launch (start us, length us, event | category | flops | bytes accessed | tf_op | source)
XLA Modules:
  0.0 693.8 jit_solution(15372378671997447707)
XLA Ops:
  6.5 0.0 all-gather.4.cloned.1.call-start
  6.5 0.7 all-gather.4.cloned.1.call-update
  7.3 0.0 all-gather.6.cloned.1.call-start
  7.3 0.7 all-gather.6.cloned.1.call-update
  8.0 0.0 all-reduce.4.cloned.1.call-start
  8.1 136.3 %all-gather.4.cloned.1.call-done = bf16[5120,1024]{1,0:T(8,128)(2,1)} async-done(((bf16[5120,128]{1,0:T(8,128)(2,1)}), bf16[5120,1024]{1,0:T(8,128)(2,1)}) %all-gather.4.cloned.1.call-update) | async-done | bytes 10485776 | tf_op jit(solution)/shard_map/all_gather | solution.py:32
  144.4 118.7 %all-gather.6.cloned.1.call-done = bf16[5120,2048]{1,0:T(8,128)(2,1)} async-done(((bf16[5120,128]{1,0:T(8,128)(2,1)}), bf16[5120,2048]{1,0:T(8,128)(2,1)}) %all-gather.6.cloned.1.call-update) | async-done | bytes 20971536 | tf_op jit(solution)/shard_map/all_gather | solution.py:35
  263.1 0.0 copy-start
  263.1 34.6 %bitcast_add_fusion = f32[1024,2048]{1,0:T(8,128)} fusion(f32[128,8,16,128]{3,2,1,0:T(8,128)} %bitcast.20, bf16[5120,1024]{1,0:T(8,128)(2,1)} %all-gather.4.cloned.1.call-done, bf16[5120,2048]{1,0:T(8,128)(2,1)} %all-gather.6.cloned.1.call-done), kind=kOutput, calls=%fused_computation.1 | convolution fusion | flops 21479030784 | bytes 48234496 | tf_op jit(solution)/shard_map/dot_general | solution.py:33
  297.8 1.5 slice_select_fusion
  299.2 0.0 all-reduce.4.cloned.1.call-update
  299.3 0.2 all-reduce.6.cloned.1.call-start
  299.5 104.5 %all-reduce.4.cloned.1.call-done = f32[128,128]{1,0:T(8,128)} async-done(((f32[128,128]{1,0:T(8,128)}), f32[128,128]{1,0:T(8,128)}) %all-reduce.4.cloned.1.call-update) | async-done | bytes 65552 | tf_op jit(solution)/shard_map/psum | solution.py:11
  404.0 0.9 copy.4
  404.9 0.9 fusion.3
  405.8 11.7 %cholesky.15 = f32[128,128]{1,0:T(8,128)S(1)} custom-call(f32[128,128]{1,0:T(8,128)S(1)} %fusion.3), custom_call_target="Cholesky" | custom-call | tf_op jit(solution)/shard_map/jit(cholesky)/cholesky | solution.py:42
  417.6 0.7 compare_reduce_fusion
  418.3 0.7 fusion.1
  419.0 9.8 %custom-call.6 = f32[1,128,128]{1,2,0:T(8,128)S(1)} custom-call(f32[1,128,128]{2,1,0:T(8,128)S(1)} %fusion.1), custom_call_target="InvertDiagBlocksLowerTriangular" | custom-call | tf_op jit(solution)/shard_map/triangular_solve | solution.py:43
  428.8 2.4 convolution_select_fusion
  431.2 0.0 all-reduce.6.cloned.1.call-update
  431.2 0.3 all-gather.8.cloned.1.call-start
  431.5 81.1 %all-reduce.6.cloned.1.call-done = f32[1024,128]{1,0:T(8,128)} async-done(((f32[1024,128]{1,0:T(8,128)}), f32[1024,128]{1,0:T(8,128)}) %all-reduce.6.cloned.1.call-update) | async-done | bytes 524304 | tf_op jit(solution)/shard_map/psum | solution.py:11
  512.6 1.5 constant_dynamic-slice_fusion
  514.0 0.0 all-gather.8.cloned.1.call-update
  514.1 0.0 copy-done
  514.1 1.2 sort.17
  515.4 34.7 %all-gather.8.cloned.1.call-done = f32[2048,128]{1,0:T(8,128)} async-done(((f32[128,128]{1,0:T(8,128)}), f32[2048,128]{1,0:T(8,128)}) %all-gather.8.cloned.1.call-update) | async-done | bytes 1048592 | tf_op jit(solution)/shard_map/all_gather | solution.py:48
  550.0 13.8 %select_select_fusion = f32[1024,2048]{1,0:T(8,128)} fusion(f32[1024,2048]{1,0:T(8,128)} %bitcast_add_fusion, f32[1024,128]{1,0:T(8,128)} %all-reduce.6.cloned.1.call-done, f32[2048,128]{1,0:T(8,128)} %all-gather.8.cloned.1.call-done, s32[1024]{0:T(1024)S(1)} %iota_add_fusion, pred[1024]{0:T(1024)(128)(4,1)S(1)} %broadcast_compare_fusion, ...), kind=kOutput, calls=%fused_computation.2 | convolution fusion | flops 3231711232 | bytes 18357248 | tf_op jit(solution)/shard_map/dot_general | solution.py:49
  563.8 7.7 %gather_fusion = f32[16,64,2048]{2,1,0:T(8,128)} fusion(f32[16,64,2048]{2,1,0:T(8,128)} %bitcast.19, s32[1024]{0:T(1024)S(1)} %pad_clamp_fusion), kind=kCustom, calls=%fused_computation | custom fusion | bytes 16777280 | tf_op jit(solution)/shard_map/jit(_take)/gather | solution.py:52
  571.5 4.3 broadcast_select_fusion
  575.8 98.0 %all_to_all.5 = f32[16,64,2048]{2,1,0:T(8,128)} all-to-all(f32[16,64,2048]{2,1,0:T(8,128)S(1)} %broadcast_select_fusion), channel_id=1, replica_groups=mesh['row'=16,'col'=8] {'row'}, dimensions={0} | all-to-all | bytes 16777216 | tf_op jit(solution)/shard_map/all_to_all | solution.py:53
  673.8 13.5 %reshape.38 = f32[16,1,64,16,1,128]{5,4,3,2,1,0:T(1,128)} reshape(f32[16,64,2048]{2,1,0:T(8,128)} %all_to_all.5) | data formatting | bytes 16777216 | tf_op jit(solution)/shard_map/reshape | solution.py:54
  (8 shorter events, 0.1 us)
Async XLA Ops:
  6.5 137.8 %all-gather.4.cloned.1.call-start = ((), (), s32[]{:S(2)}) async-start(), calls=%async_computation.1 | async-start | bytes 11796480 | tf_op jit(solution)/shard_map/all_gather | solution.py:32
  7.3 255.9 %all-gather.6.cloned.1.call-start = ((), (), s32[]{:S(2)}) async-start(), calls=%async_computation.2 | async-start | bytes 22282240 | tf_op jit(solution)/shard_map/all_gather | solution.py:35
  8.0 396.0 %all-reduce.4.cloned.1.call-start = ((), (), s32[]{:S(2)}) async-start(), calls=%async_computation.3 | async-start | bytes 131072 | tf_op jit(solution)/shard_map/psum | solution.py:11
  263.1 250.9 %copy-start = (s32[16]{0:T(128)S(1)}, s32[16]{0:T(128)}, u32[]{:S(2)}) copy-start(s32[16]{0:T(128)} %param.5) | copy-start | bytes 196
  299.3 213.3 %all-reduce.6.cloned.1.call-start = ((), (), s32[]{:S(2)}) async-start(), calls=%async_computation.4 | async-start | bytes 1048576 | tf_op jit(solution)/shard_map/psum | solution.py:11
  431.2 118.8 %all-gather.8.cloned.1.call-start = ((), (), s32[]{:S(2)}) async-start(), calls=%async_computation.5 | async-start | bytes 1114112 | tf_op jit(solution)/shard_map/all_gather | solution.py:48
Sparse Core Ops, SparseCore 0:
  9.5 134.8 all-gather.3
  146.0 117.0 all-gather.5
  299.4 104.5 all-reduce.3
  431.3 81.2 all-reduce.5
  514.2 35.8 all-gather.7
where the time goes:
time: 695 us; the launch traced here: 694 us
  waiting for transfers between devices  477 us (69%)
  blocking collectives  98 us (14%)
  matrix products  50.8 us (7%)
  other arithmetic  30.9 us (4%)
  local copies, waits for them, and re-layouts  23.6 us (3%)
  between operations  13.2 us (2%)
    psum x2, waiting for transfers between devices, broadcast(): return lax.psum(jnp.where(mine, array, jnp.zeros_like(array)), axis)  186 us
    all_gather x1, waiting for transfers between devices, on_device(): mine_rows = lax.all_gather(genotypes, 'col', axis=1, tiled=True)  136 us
    all_gather x1, waiting for transfers between devices, on_device(): lax.all_gather(genotypes, 'row', axis=1, tiled=True)  119 us
    all_to_all x1, blocking collectives, on_device(): lax.all_to_all(send_tiles, 'row', split_axis=0, concat_axis=0, tiled=True)  98 us
    all_gather x1, waiting for transfers between devices, on_device(): col_factor = lax.all_gather(col_slice, 'row', axis=0, tiled=True)  34.7 us
    dot_general x1, matrix products, on_device(): lax.dot_general(mine_rows, lax.all_gather(genotypes, 'row', axis=1, tiled...  34.6 us
  transfers between devices with their start and end apart: 5, of which 5 were waited for; matrix products, arithmetic and copies ran while one was open for 0% of the time, Pallas kernels for 0%

commit v1 on v0

--- a/solution.py
+++ b/solution.py
@@ -2,13 +2,14 @@
 import jax.numpy as jnp
 from jax import lax
 from jax.sharding import PartitionSpec as P
+from jax.lax import all_gather
 
 NB = 128
 
 
 def broadcast(array, axis, root):
     mine = lax.axis_index(axis) == root
-    return lax.psum(jnp.where(mine, array, jnp.zeros_like(array)), axis)
+    return all_gather(jnp.where(mine, array, jnp.zeros_like(array)), axis).sum(axis=0)
 
 
 def assemble(trail, row_factor, global_rows, col_index, col_width):

time: 695 us -> 605 us (0.87)
  waiting for transfers between devices: 477 us -> 388 us
    psum x2 -> x0, waiting for transfers between devices: 186 us -> none  [broadcast(): return lax.psum(jnp.where(mine, array, jnp.zeros_like(array)), axis)]
    all_gather x0 -> x2, waiting for transfers between devices: none -> 101 us  [broadcast(): all_gather(jnp.where(mine, array, jnp.zeros_like(array)), axis).sum(axis=0)]
where the time goes in v1:
time: 605 us; the launch traced here: 604 us
  waiting for transfers between devices  388 us (64%)
  blocking collectives  98 us (16%)
  matrix products  48.7 us (8%)
  other arithmetic  33.8 us (6%)
  local copies, waits for them, and re-layouts  21.9 us (4%)
  between operations  13.3 us (2%)
    all_gather x1, waiting for transfers between devices, on_device(): mine_rows = lax.all_gather(genotypes, 'col', axis=1, tiled=True)  136 us
    all_gather x1, waiting for transfers between devices, on_device(): lax.all_gather(genotypes, 'row', axis=1, tiled=True)  119 us
    all_gather x2, waiting for transfers between devices, broadcast(): all_gather(jnp.where(mine, array, jnp.zeros_like(array)), axis).sum(axis=0)  101 us
    all_to_all x1, blocking collectives, on_device(): lax.all_to_all(send_tiles, 'row', split_axis=0, concat_axis=0, tiled=True)  98 us
    dot_general x1, matrix products, on_device(): lax.dot_general(mine_rows, lax.all_gather(genotypes, 'row', axis=1, tiled...  34.6 us
    all_gather x1, waiting for transfers between devices, on_device(): col_factor = lax.all_gather(col_slice, 'row', axis=0, tiled=True)  30.2 us
    reshape x1, local copies, waits for them, and re-layouts, on_device(): return result.reshape(rows_count, 1, sub_rows, rows_count, 1, shard_cols)  13.5 us
    another operation x3, other arithmetic, on_device(): lower_factor = jnp.linalg.cholesky(leading)  12.5 us
  transfers between devices with their start and end apart: 5, of which 5 were waited for; matrix products, arithmetic and copies ran while one was open for 0% of the time, Pallas kernels for 0%

profile of v1, /device:TPU:1, one launch (start us, length us, event | category | flops | bytes accessed | tf_op | source)
XLA Modules:
  0.0 604.0 jit_solution(14833847625136259112)
XLA Ops:
  6.5 0.0 all-gather.8.cloned.1.call-start
  6.5 0.7 all-gather.8.cloned.1.call-update
  7.3 0.0 all-gather.10.cloned.1.call-start
  7.3 0.7 all-gather.10.cloned.1.call-update
  8.0 0.0 all-gather.14.cloned.1.call-start
  8.1 136.3 %all-gather.8.cloned.1.call-done = bf16[5120,1024]{1,0:T(8,128)(2,1)} async-done(((bf16[5120,128]{1,0:T(8,128)(2,1)}), bf16[5120,1024]{1,0:T(8,128)(2,1)}) %all-gather.8.cloned.1.call-update) | async-done | bytes 10485776 | tf_op jit(solution)/shard_map/all_gather | solution.py:33
  144.4 118.7 %all-gather.10.cloned.1.call-done = bf16[5120,2048]{1,0:T(8,128)(2,1)} async-done(((bf16[5120,128]{1,0:T(8,128)(2,1)}), bf16[5120,2048]{1,0:T(8,128)(2,1)}) %all-gather.10.cloned.1.call-update) | async-done | bytes 20971536 | tf_op jit(solution)/shard_map/all_gather | solution.py:36
  263.1 34.6 %bitcast_add_fusion = f32[1024,2048]{1,0:T(8,128)} fusion(f32[128,8,16,128]{3,2,1,0:T(8,128)} %bitcast.24, bf16[5120,1024]{1,0:T(8,128)(2,1)} %all-gather.8.cloned.1.call-done, bf16[5120,2048]{1,0:T(8,128)(2,1)} %all-gather.10.cloned.1.call-done), kind=kOutput, calls=%fused_computation.1 | convolution fusion | flops 21479030784 | bytes 48234496 | tf_op jit(solution)/shard_map/dot_general | solution.py:34
  297.7 0.0 copy-start
  297.7 1.5 slice_select_fusion
  299.2 0.0 all-gather.14.cloned.1.call-update
  299.2 0.2 all-gather.16.cloned.1.call-start
  299.5 31.4 %all-gather.14.cloned.1.call-done = f32[2048,128]{1,0:T(8,128)} async-done(((f32[128,128]{1,0:T(8,128)}), f32[2048,128]{1,0:T(8,128)}) %all-gather.14.cloned.1.call-update) | async-done | bytes 1048592 | tf_op jit(solution)/shard_map/all_gather | solution.py:12
  330.9 1.3 reduce_sum.18
  332.1 0.1 copy.5
  332.3 11.7 %cholesky.15 = f32[128,128]{1,0:T(8,128)S(1)} custom-call(f32[128,128]{1,0:T(8,128)S(1)} %fusion.3), custom_call_target="Cholesky" | custom-call | tf_op jit(solution)/shard_map/jit(cholesky)/cholesky | solution.py:43
  344.0 0.7 compare_reduce_fusion
  344.7 0.7 fusion.1
  345.4 9.8 %custom-call.6 = f32[1,128,128]{1,2,0:T(8,128)S(1)} custom-call(f32[1,128,128]{2,1,0:T(8,128)S(1)} %fusion.1), custom_call_target="InvertDiagBlocksLowerTriangular" | custom-call | tf_op jit(solution)/shard_map/triangular_solve | solution.py:44
  355.2 2.4 convolution_select_fusion
  357.7 0.0 all-gather.16.cloned.1.call-update
  357.7 0.0 all-gather.12.cloned.1.call-start
  357.7 69.9 %all-gather.16.cloned.1.call-done = f32[8192,128]{1,0:T(8,128)} async-done(((f32[1024,128]{1,0:T(8,128)}), f32[8192,128]{1,0:T(8,128)}) %all-gather.16.cloned.1.call-update) | async-done | bytes 4194320 | tf_op jit(solution)/shard_map/all_gather | solution.py:12
  427.6 2.4 reduce_sum.19
  430.1 0.6 constant_dynamic-slice_fusion
  430.7 0.0 all-gather.12.cloned.1.call-update
  430.7 0.0 copy-done
  430.7 1.2 sort.17
  432.0 30.2 %all-gather.12.cloned.1.call-done = f32[2048,128]{1,0:T(8,128)} async-done(((f32[128,128]{1,0:T(8,128)}), f32[2048,128]{1,0:T(8,128)}) %all-gather.12.cloned.1.call-update) | async-done | bytes 1048592 | tf_op jit(solution)/shard_map/all_gather | solution.py:49
  462.2 11.7 %select_select_fusion = f32[1024,2048]{1,0:T(8,128)} fusion(f32[1024,2048]{1,0:T(8,128)} %bitcast_add_fusion, f32[1024,128]{1,0:T(8,128)S(1)} %reduce_sum.19, f32[2048,128]{1,0:T(8,128)} %all-gather.12.cloned.1.call-done, s32[1024]{0:T(1024)S(1)} %iota_add_fusion, pred[1024]{0:T(1024)(128)(4,1)S(1)} %broadcast_compare_fusion, pred[2048]{0:T(1024)(128)(4,1)S(1)} %fusion.4), kind=kOutput, calls=%fused_computation.2 | convolution fusion | flops 3231711232 | bytes 18357248 | tf_op jit(solution)/shard_map/dot_general | solution.py:50
  473.9 7.7 %gather_fusion = f32[16,64,2048]{2,1,0:T(8,128)} fusion(f32[16,64,2048]{2,1,0:T(8,128)} %bitcast.21, s32[1024]{0:T(1024)S(1)} %pad_clamp_fusion), kind=kCustom, calls=%fused_computation | custom fusion | bytes 16777280 | tf_op jit(solution)/shard_map/jit(_take)/gather | solution.py:53
  481.6 4.3 broadcast_select_fusion
  486.0 98.0 %all_to_all.5 = f32[16,64,2048]{2,1,0:T(8,128)} all-to-all(f32[16,64,2048]{2,1,0:T(8,128)S(1)} %broadcast_select_fusion), channel_id=1, replica_groups=mesh['row'=16,'col'=8] {'row'}, dimensions={0} | all-to-all | bytes 16777216 | tf_op jit(solution)/shard_map/all_to_all | solution.py:54
  584.0 13.5 %reshape.38 = f32[16,1,64,16,1,128]{5,4,3,2,1,0:T(1,128)} reshape(f32[16,64,2048]{2,1,0:T(8,128)} %all_to_all.5) | data formatting | bytes 16777216 | tf_op jit(solution)/shard_map/reshape | solution.py:55
  (9 shorter events, 0.1 us)
Async XLA Ops:
  6.5 137.8 %all-gather.8.cloned.1.call-start = ((), (), s32[]{:S(2)}) async-start(), calls=%async_computation.1 | async-start | bytes 11796480 | tf_op jit(solution)/shard_map/all_gather | solution.py:33
  7.3 255.9 %all-gather.10.cloned.1.call-start = ((), (), s32[]{:S(2)}) async-start(), calls=%async_computation.2 | async-start | bytes 22282240 | tf_op jit(solution)/shard_map/all_gather | solution.py:36
  8.0 322.8 %all-gather.14.cloned.1.call-start = ((), (), s32[]{:S(2)}) async-start(), calls=%async_computation.4 | async-start | bytes 1114112 | tf_op jit(solution)/shard_map/all_gather | solution.py:12
  297.7 133.0 %copy-start = (s32[16]{0:T(128)S(1)}, s32[16]{0:T(128)}, u32[]{:S(2)}) copy-start(s32[16]{0:T(128)} %param.5) | copy-start | bytes 196
  299.2 128.4 %all-gather.16.cloned.1.call-start = ((), (), s32[]{:S(2)}) async-start(), calls=%async_computation.5 | async-start | bytes 4718592 | tf_op jit(solution)/shard_map/all_gather | solution.py:12
  357.7 104.6 %all-gather.12.cloned.1.call-start = ((), (), s32[]{:S(2)}) async-start(), calls=%async_computation.3 | async-start | bytes 1114112 | tf_op jit(solution)/shard_map/all_gather | solution.py:49
Sparse Core Ops, SparseCore 0:
  9.5 134.8 all-gather.7
  146.0 117.0 all-gather.9
  299.4 31.4 all-gather.13
  357.8 69.7 all-gather.15
  430.8 31.3 all-gather.11
